TPU v7x, 256 devices: a whole 4x4x8 slice. The times are simulated.
256 devices in a mesh: sample: 16 (over z, core), expert: 16 (over y, x).
Axes of the slice: x: 4, y: 4, z: 8, core: 2. Of those that a mesh axis runs over, the one named last changes fastest.
Arguments:
- queries: bfloat16 [128, 16, 8192], P('expert', 'sample'), may hold values from -8 to 8
- prompt_kv: bfloat16 [128, 1024, 1024], P('expert', 'sample'), may hold values from -8 to 8
- gen_kv: bfloat16 [128, 16, 32, 1024], P('expert', 'sample'), may hold values from -4 to 4
- gen_lengths: int32 [128, 16], P('expert', 'sample'), may hold values from 1 to 32, 256 in all within a row
- out_proj: bfloat16 [8192, 4096], P(None, 'sample'), may hold values from -1 to 1
- residual: bfloat16 [128, 16, 4096], P('expert', None, 'sample'), may hold values from -160 to 160
- norm_gain: float32 [4096], P('sample'), may hold values from 0.1 to 1.9
- w_gate_up: bfloat16 [48, 4096, 3072], P('expert', 'sample'), may hold values from -0.09375 to 0.09375
- w_down: bfloat16 [48, 1536, 4096], P('expert', None, 'sample'), may hold values from -0.15625 to 0.15625
- routes: int32 [128, 16, 8], P('expert'), may hold values from 0 to 47, all different within a row; in each aligned block of 128 rows (0 to 127, 128 to 255, ..., all dimensions but the last counted through in order) at most 26 rows name the same one
- route_probs: float32 [128, 16, 8], P('expert'), may hold values from 0.1 to 1
Outputs:
- mixed: bfloat16 [128, 16, 4096], P('expert', None, 'sample')
- expert_out: bfloat16 [128, 16, 4096], P('expert', None, 'sample')
Inputs may be any that keep to these rules, and one draw needn't show every extreme that they name: `gen_lengths`: in each prompt, at least one sample has 32 generated tokens. `routes`: each row names 8 different experts. Among the 128 rows of the prompts of one index of expert, no expert is named by more than 26 rows, a bound that some block reaches.
All inputs are finite; a program needn't handle non-finite values. No bound on the sum of `gen_lengths` on one device may be relied on, other than what follows from the above.
Results may differ from a plain program's by a relative error of at most 0.028.
Values may be sent and summed in bfloat16 or wider, within the bound.
A program may use at most 128 MiB of HBM per device.

v0:
```python
import jax
import jax.numpy as jnp
from jax import lax
from jax.sharding import PartitionSpec as P

D = 4096
FF = 1536
QHEADS = 64
KVHEADS = 4
HDIM = 128
TOPK = 8
EXP_COL = 3
NEGATIVE = -1e30
EPSILON = 1e-06


def absorb(carried, scores, value_rows):
    highest = jnp.maximum(carried[0], jnp.max(scores, axis=-1))
    rescale = jnp.exp(carried[0] - highest)
    weights = jnp.exp(scores - highest[..., None])
    weight_sum = carried[1] * rescale + jnp.sum(weights, axis=-1)
    numerator = carried[2] * rescale[..., None] + jnp.einsum(
        "brhgn,bnhd->brhgd",
        weights,
        value_rows.astype(jnp.float32),
        precision=lax.Precision.HIGHEST,
    )
    return (highest, weight_sum, numerator)


def split_cache(cache):
    kv_width = KVHEADS * HDIM
    prompts_here = cache.shape[0]
    length = cache.shape[1]
    key_rows = cache[:, :, :kv_width].reshape(prompts_here, length, KVHEADS, HDIM)
    value_rows = cache[:, :, kv_width:].reshape(prompts_here, length, KVHEADS, HDIM)
    return (key_rows, value_rows)


def score_rows(query, key_rows):
    return jnp.einsum(
        "brhgd,bnhd->brhgn", query, key_rows, preferred_element_type=jnp.float32
    ) * HDIM ** (-0.5)


def empty_state(shape):
    return (
        jnp.full(shape, NEGATIVE, jnp.float32),
        jnp.zeros(shape, jnp.float32),
        jnp.zeros(shape + (HDIM,), jnp.float32),
    )


def on_device(
    queries,
    prompt_kv,
    gen_kv,
    gen_lengths,
    out_proj,
    residual,
    norm_gain,
    w_gate_up,
    w_down,
    routes,
    route_probs,
):
    prompts_here = queries.shape[0]
    groups = QHEADS // KVHEADS
    samples = lax.axis_size("sample")
    width = residual.shape[2]
    own_query = queries.reshape(prompts_here, 1, KVHEADS, groups, HDIM)
    gen_keys, gen_values = split_cache(gen_kv[:, 0])
    positions = jnp.arange(gen_kv.shape[2], dtype=jnp.int32)
    valid = (positions[None, :] < gen_lengths)[:, None, None, None, :]
    gen_scores = jnp.where(valid, score_rows(own_query, gen_keys), NEGATIVE)
    own_state = absorb(empty_state((prompts_here, 1, KVHEADS, groups)), gen_scores, gen_values)
    key_rows, value_rows = split_cache(lax.all_gather(prompt_kv, "sample", axis=1, tiled=True))
    merged = absorb(own_state, score_rows(own_query, key_rows), value_rows)
    attended = (
        (merged[2] / merged[1][..., None])
        .astype(jnp.bfloat16)
        .reshape(prompts_here, 1, QHEADS * HDIM)
    )
    projected = jnp.einsum(
        "bnq,qd->bnd",
        lax.all_gather(attended, "sample", axis=1, tiled=True),
        out_proj,
        preferred_element_type=jnp.float32,
    )
    mixed = projected.astype(jnp.bfloat16)
    stream = residual.astype(jnp.float32) + projected
    squares = lax.psum(jnp.sum(stream * stream, axis=-1), "sample")
    factor = lax.rsqrt(squares / D + EPSILON)
    row_count = prompts_here * samples
    normed = (stream * factor[..., None] * norm_gain).astype(jnp.bfloat16).reshape(row_count, width)
    owners = lax.axis_size("expert")
    experts_all = EXP_COL * owners
    capacity = 5 * prompts_here * samples * TOPK // (4 * experts_all)
    expert_ids = routes.reshape(row_count, TOPK)
    route_weight = route_probs.reshape(row_count, TOPK)
    expert_hits = jnp.sum(
        (expert_ids[:, :, None] == jnp.arange(experts_all, dtype=jnp.int32)[None, None, :]).astype(
            jnp.int32
        ),
        axis=1,
    )
    before = jnp.cumsum(expert_hits, axis=0) - expert_hits
    arrival = jnp.take_along_axis(before, expert_ids, axis=1)
    slot_index = (expert_ids * capacity + arrival).reshape(-1)
    outgoing = (
        jnp.zeros((experts_all * capacity, width), jnp.bfloat16)
        .at[slot_index]
        .set(jnp.repeat(normed, TOPK, axis=0))
    )
    outgoing = outgoing.reshape(owners, EXP_COL, capacity, width)
    partial_sums = jnp.einsum(
        "sjcd,jdf->sjcf",
        lax.all_to_all(outgoing, "expert", split_axis=0, concat_axis=0, tiled=True),
        w_gate_up,
        preferred_element_type=jnp.float32,
    )
    gate_up = lax.psum(partial_sums.astype(jnp.bfloat16), "sample").astype(jnp.float32)
    activated = (jax.nn.silu(gate_up[..., :FF]) * gate_up[..., FF:]).astype(jnp.bfloat16)
    finished = jnp.einsum(
        "sjcf,jfd->sjcd", activated, w_down, preferred_element_type=jnp.float32
    ).astype(jnp.bfloat16)
    returned = lax.all_to_all(finished, "expert", split_axis=0, concat_axis=0, tiled=True)
    picked = jnp.take(returned.reshape(experts_all * capacity, width), slot_index, axis=0).reshape(
        row_count, TOPK, width
    )
    combined = jnp.sum(picked.astype(jnp.float32) * route_weight[:, :, None], axis=1)
    expert_out = combined.astype(jnp.bfloat16).reshape(prompts_here, samples, width)
    return (mixed, expert_out)


def solution(mesh):
    placed = (
        P("expert", "sample", None),
        P("expert", "sample", None),
        P("expert", "sample", None, None),
        P("expert", "sample"),
        P(None, "sample"),
        P("expert", None, "sample"),
        P("sample"),
        P("expert", "sample", None),
        P("expert", None, "sample"),
        P("expert", None, None),
        P("expert", None, None),
    )
    return jax.shard_map(
        on_device,
        mesh=mesh,
        in_specs=placed,
        out_specs=(P("expert", None, "sample"), P("expert", None, "sample")),
        check_vma=False,
    )
```

profile of v0, /device:TPU:97, one launch (start us, length us, event | category | flops | bytes accessed | tf_op | source)
XLA Modules:
  0.0 452.4 jit_solution(12887853357959558005)
XLA Ops:
  7.2 2.9 copy.82
  10.2 0.7 iota_compare_fusion.1
  11.0 1.1 slice_bitcast_fusion
  12.0 1.2 fusion.59
  13.3 94.0 %all-gather.3.cloned.1.call-done = bf16[8,1024,1024]{2,0,1:T(8,128)(2,1)} async-done(((bf16[8,64,1024]{2,0,1:T(8,128)(2,1)}), bf16[8,1024,1024]{2,0,1:T(8,128)(2,1)}) %all-gather.3.cloned.1.call-update) | async-done | bytes 16777232 | tf_op jit(solution)/shard_map/all_gather | solution.py:77
  107.3 11.3 %fusion.58 = (bf16[8,1024,512]{2,0,1:T(8,128)(2,1)}, bf16[8,1024,512]{2,0,1:T(8,128)(2,1)}) fusion(bf16[8,1024,1024]{2,0,1:T(8,128)(2,1)} %all-gather.3.cloned.1.call-done), kind=kLoop, calls=%fused_computation.79 | loop fusion | bytes 33554432 | tf_op jit(solution)/shard_map/slice | solution.py:35
  118.6 12.3 %copy.109 = bf16[8,1024,512]{1,2,0:T(8,128)(2,1)} copy(bf16[8,1024,512]{2,0,1:T(8,128)(2,1)} %get-tuple-element.8) | data formatting | bytes 16777216
  130.9 6.0 %bitcast_reduce_fusion = (f32[8,4,16]{2,1,0:T(4,128)S(1)}, f32[8,4,1024,16]{2,3,1,0:T(8,128)}) fusion(bf16[8,1024,4,128]{1,3,2,0:T(8,128)(2,1)} %bitcast.118, bf16[8,4,16,128]{3,0,2,1:T(8,128)(2,1)S(1)} %bitcast.124), kind=kOutput, calls=%fused_computation.14 | convolution fusion | flops 135265792 | bytes 10618880 | tf_op jit(solution)/shard_map/brhgd,bnhd->brhgn/dot_general | solution.py:41
  136.8 12.2 %copy.110 = bf16[8,1024,512]{1,2,0:T(8,128)(2,1)} copy(bf16[8,1024,512]{2,0,1:T(8,128)(2,1)} %get-tuple-element.9) | data formatting | bytes 16777216
  149.1 2.2 fusion.10
  151.4 9.0 %fusion.22 = f32[8,4,128,1,16]{2,4,1,0,3:T(8,128)S(1)} fusion(bf16[8,1024,4,128]{1,3,2,0:T(8,128)(2,1)} %bitcast.117, f32[8,4,1024,16]{2,3,1,0:T(8,128)S(1)} %copy-done.1, f32[8,4,16]{2,1,0:T(4,128)S(1)} %get-tuple-element.15), kind=kOutput, calls=%fused_computation.19 | convolution fusion | flops 806354944 | bytes 10749952 | tf_op jit(solution)/shard_map/brhgn,bnhd->brhgd/dot_general | solution.py:22
  160.7 0.4 fusion.33
  161.2 0.7 reshape.292
  162.9 7.1 %gather_fusion.1 = s32[1024]{0:T(1024)S(1)} fusion(s32[128,48]{1,0:T(8,128)S(1)} %sub.53, s32[1024]{0:T(1024)S(1)} %reshape.308), kind=kCustom, calls=%fused_computation.1 | custom fusion | bytes 16384 | tf_op jit(solution)/shard_map/jit(take_along_axis)/gather | solution.py:108
  170.0 30.0 %all-gather.5.cloned.1.call-done = bf16[8,16,8192]{2,0,1:T(8,128)(2,1)} async-done(((bf16[8,1,8192]{2,0,1:T(8,128)(2,1)}), bf16[8,16,8192]{2,0,1:T(8,128)(2,1)}) %all-gather.5.cloned.1.call-update) | async-done | bytes 2097168 | tf_op jit(solution)/shard_map/all_gather | solution.py:86
  200.0 3.6 multiply_reduce_fusion.1
  203.6 23.5 %psum.14 = f32[8,16]{0,1:T(8,128)S(1)} all-reduce(f32[8,16]{0,1:T(8,128)S(1)} %get-tuple-element.21), channel_id=1, replica_groups=mesh['sample'=16,'expert'=16] {'sample'}, use_global_device_ids=true, to_apply=%region_7.8 | all-reduce | flops 128 | bytes 1024 | tf_op jit(solution)/shard_map/psum | solution.py:92
  227.3 5.8 %scatter_custom_fusion = bf16[1248,256]{1,0:T(8,128)(2,1)} fusion(s32[1024]{0:T(1024)S(1)} %bitcast.126, bf16[]{:T(256)} %constant.35.clone.1, bf16[128,256]{1,0:T(8,128)(2,1)S(1)} %bitcast.121), kind=kCustom, calls=%fused_computation.36 | custom fusion | bytes 704514 | tf_op jit(solution)/shard_map/scatter | solution.py:113
  233.1 1.3 reshape.298
  234.3 21.4 %all_to_all.10 = bf16[16,3,26,256]{3,2,1,0:T(8,128)(2,1)S(1)} all-to-all(bf16[16,3,26,256]{3,2,1,0:T(8,128)(2,1)S(1)} %reshape.298), channel_id=1, replica_groups=mesh['sample'=16,'expert'=16] {'expert'}, dimensions={0} | all-to-all | bytes 1277952 | tf_op jit(solution)/shard_map/all_to_all | solution.py:118
  255.7 7.5 %convert_bitcast_fusion = bf16[16,3,26,3072]{3,2,0,1:T(8,128)(2,1)} fusion(bf16[3,256,3072]{2,1,0:T(8,128)(2,1)} %param.18, bf16[16,3,26,256]{3,2,1,0:T(8,128)(2,1)S(1)} %all_to_all.10), kind=kOutput, calls=%fused_computation.5 | convolution fusion | flops 1966768128 | bytes 13025280 | tf_op jit(solution)/shard_map/sjcd,jdf->sjcf/dot_general | solution.py:116
  263.2 133.9 %all-reduce.2.cloned.1.call-done = bf16[16,3,26,3072]{3,2,0,1:T(8,128)(2,1)} async-done(((bf16[16,3,26,3072]{3,2,0,1:T(8,128)(2,1)}), bf16[16,3,26,3072]{3,2,0,1:T(8,128)(2,1)}) %all-reduce.2.cloned.1.call-update) | async-done | bytes 7667728 | tf_op jit(solution)/shard_map/psum | solution.py:122
  397.1 12.4 %convert_element_type.49 = f32[16,3,26,3072]{3,2,0,1:T(8,128)} convert(bf16[16,3,26,3072]{3,2,0,1:T(8,128)(2,1)} %all-reduce.2.cloned.1.call-done) | non-fusion elementwise | flops 3833856 | bytes 23003136 | tf_op jit(solution)/shard_map/convert_element_type | solution.py:122
  409.6 8.0 %fusion.17 = bf16[16,3,26,256]{3,2,0,1:T(8,128)(2,1)S(1)} fusion(bf16[3,1536,256]{2,1,0:T(8,128)(2,1)S(1)} %copy-done, f32[16,3,26,3072]{3,2,0,1:T(8,128)} %convert_element_type.49), kind=kOutput, calls=%fused_computation.18 | convolution fusion | flops 993288192 | bytes 18333696 | tf_op jit(solution)/shard_map/sjcf,jfd->sjcd/dot_general | solution.py:124
  417.6 1.0 copy.99
  418.5 6.6 %all-to-all-start.1 = ((bf16[16,3,26,256]{3,2,1,0:T(8,128)(2,1)}), bf16[16,3,26,256]{3,2,1,0:T(8,128)(2,1)}, u32[]{:S(2)}, u32[]{:S(2)}) async-start(bf16[16,3,26,256]{3,2,1,0:T(8,128)(2,1)} %copy.99), calls=%async_computation.1 | async-start | bytes 1572864 | tf_op jit(solution)/shard_map/all_to_all | solution.py:127
  425.4 0.7 copy.107
  426.1 0.6 copy.102
  426.7 11.9 %all-to-all-done.1 = bf16[16,3,26,256]{3,2,1,0:T(8,128)(2,1)} async-done(((bf16[16,3,26,256]{3,2,1,0:T(8,128)(2,1)}), bf16[16,3,26,256]{3,2,1,0:T(8,128)(2,1)}, u32[]{:S(2)}, u32[]{:S(2)}) %all-to-all-start.1) | async-done | bytes 639008 | tf_op jit(solution)/shard_map/all_to_all | solution.py:127
  438.7 1.3 reshape.299
  440.0 3.9 gather_fusion
  443.9 1.9 multiply_reduce_fusion
  (44 shorter events, 1.8 us)
Async XLA Ops:
  7.2 402.4 %copy-start = (bf16[3,1536,256]{2,1,0:T(8,128)(2,1)S(1)}, bf16[3,1536,256]{2,1,0:T(8,128)(2,1)}, u32[]{:S(2)}) copy-start(bf16[3,1536,256]{2,1,0:T(8,128)(2,1)} %param.19) | copy-start | bytes 7077892
  7.2 100.1 %all-gather.3.cloned.1.call-start = ((), (), s32[]{:S(2)}) async-start(), calls=%async_computation.2 | async-start | bytes 17825792 | tf_op jit(solution)/shard_map/all_gather | solution.py:77
  10.2 189.8 %all-gather.5.cloned.1.call-start = ((), (), s32[]{:S(2)}) async-start(), calls=%async_computation.3 | async-start | bytes 2228224 | tf_op jit(solution)/shard_map/all_gather | solution.py:86
  118.6 12.3 %copy-start.3 = (bf16[8,1,8192]{2,0,1:T(8,128)(2,1)S(1)}, bf16[8,1,8192]{2,0,1:T(8,128)(2,1)}, u32[]{:S(2)}) copy-start(bf16[8,1,8192]{2,0,1:T(8,128)(2,1)} %param.11) | copy-start | bytes 393220
  149.1 2.3 copy-start.1
  151.4 10.6 %copy-start.4 = (s32[8,16,8]{1,2,0:T(8,128)S(1)}, s32[8,16,8]{1,2,0:T(8,128)}, u32[]{:S(2)}) copy-start(s32[8,16,8]{1,2,0:T(8,128)} %param.20) | copy-start | bytes 12292
  161.9 235.2 %all-reduce.2.cloned.1.call-start = ((), (), s32[]{:S(2)}) async-start(), calls=%async_computation.4 | async-start | bytes 18874368 | tf_op jit(solution)/shard_map/psum | solution.py:122
  162.8 37.2 %copy-start.2 = (bf16[8,16,256]{2,1,0:T(8,128)(2,1)S(1)}, bf16[8,16,256]{2,1,0:T(8,128)(2,1)}, u32[]{:S(2)}) copy-start(bf16[8,16,256]{2,1,0:T(8,128)(2,1)} %param.16) | copy-start | bytes 196612
  169.9 57.2 %copy-start.6 = (f32[256]{0:T(256)S(1)}, f32[256]{0:T(256)}, u32[]{:S(2)}) copy-start(f32[256]{0:T(256)} %param.17) | copy-start | bytes 3076
  409.6 15.8 %copy-start.5 = (f32[8,16,8]{1,2,0:T(8,128)S(1)}, f32[8,16,8]{1,2,0:T(8,128)}, u32[]{:S(2)}) copy-start(f32[8,16,8]{1,2,0:T(8,128)} %param.21) | copy-start | bytes 12292
  418.5 20.2 %all-to-all-start.1 = ((bf16[16,3,26,256]{3,2,1,0:T(8,128)(2,1)}), bf16[16,3,26,256]{3,2,1,0:T(8,128)(2,1)}, u32[]{:S(2)}, u32[]{:S(2)}) async-start(bf16[16,3,26,256]{3,2,1,0:T(8,128)(2,1)} %copy.99), calls=%async_computation.1 | async-start | bytes 1572864 | tf_op jit(solution)/shard_map/all_to_all | solution.py:127
Sparse Core Ops, SparseCore 0:
  10.3 96.8 all-gather.2
  162.0 37.9 all-gather.4
  263.3 133.7 all-reduce.1
where the time goes:
time: 453 us; the launch traced here: 452 us
  waiting for transfers between devices  270 us (60%)
  local copies, waits for them, and re-layouts  63.1 us (14%)
  blocking collectives  44.9 us (10%)
  matrix products  35.7 us (8%)
  other arithmetic  18.1 us (4%)
  between operations  14 us (3%)
  starting transfers between devices  6.69 us (1%)
    psum x1, waiting for transfers between devices, on_device(): lax.psum(partial_sums.astype(jnp.bfloat16), 'sample').astype(jnp.float32)  134 us
    all_gather x1, waiting for transfers between devices, on_device(): lax.all_gather(prompt_kv, 'sample', axis=1, tiled=True)  94 us
    all_gather x1, waiting for transfers between devices, on_device(): lax.all_gather(attended, 'sample', axis=1, tiled=True)  30 us
    unnamed x21, local copies, waits for them, and re-layouts  29.3 us
    psum x1, blocking collectives, on_device(): squares = lax.psum(jnp.sum(stream * stream, axis=-1), 'sample')  23.5 us
    all_to_all x1, blocking collectives, on_device(): lax.all_to_all(outgoing, 'expert', split_axis=0, concat_axis=0, tiled=True)  21.4 us
    convert_element_type x1, other arithmetic, on_device(): lax.psum(partial_sums.astype(jnp.bfloat16), 'sample').astype(jnp.float32)  12.4 us
    all_to_all x1, waiting for transfers between devices, on_device(): lax.all_to_all(finished, 'expert', split_axis=0, concat_axis=0, tiled=True)  11.9 us
  transfers between devices with their start and end apart: 4, of which 4 were waited for; matrix products, arithmetic and copies ran while one was open for 3% of the time, Pallas kernels for 0%

commit v1 on v0

--- a/solution.py
+++ b/solution.py
@@ -83,7 +83,9 @@
     )
     projected = jnp.einsum(
         "bnq,qd->bnd",
-        lax.all_gather(attended, "sample", axis=1, tiled=True),
+        jnp.concatenate(
+            lax.all_to_all(jnp.stack([attended] * lax.axis_size("sample")), "sample", 0, 0), axis=1
+        ),
         out_proj,
         preferred_element_type=jnp.float32,
     )

time: 453 us -> 471 us (1.040)
  waiting for transfers between devices: 270 us -> 281 us
  starting transfers between devices: 6.69 us -> 11.8 us
    all_to_all x0 -> x1, waiting for transfers between devices: none -> 40.7 us  [on_device(): lax.all_to_all(jnp.stack([attended] * lax.axis_size('sample')), 'sample',...]
    all_gather x1 -> x0, waiting for transfers between devices: 30 us -> none  [on_device(): lax.all_gather(attended, 'sample', axis=1, tiled=True)]
    all_to_all x0 -> x1, starting transfers between devices: none -> 5.16 us  [on_device(): lax.all_to_all(jnp.stack([attended] * lax.axis_size('sample')), 'sample',...]
where the time goes in v1:
time: 471 us; the launch traced here: 470 us
  waiting for transfers between devices  281 us (60%)
  local copies, waits for them, and re-layouts  63.9 us (14%)
  blocking collectives  44.9 us (10%)
  matrix products  35.7 us (8%)
  other arithmetic  18.1 us (4%)
  between operations  14.3 us (3%)
  starting transfers between devices  11.8 us (3%)
    psum x1, waiting for transfers between devices, on_device(): lax.psum(partial_sums.astype(jnp.bfloat16), 'sample').astype(jnp.float32)  134 us
    all_gather x1, waiting for transfers between devices, on_device(): lax.all_gather(prompt_kv, 'sample', axis=1, tiled=True)  94 us
    all_to_all x1, waiting for transfers between devices, on_device(): lax.all_to_all(jnp.stack([attended] * lax.axis_size('sample')), 'sample',...  40.7 us
    unnamed x21, local copies, waits for them, and re-layouts  29.3 us
    psum x1, blocking collectives, on_device(): squares = lax.psum(jnp.sum(stream * stream, axis=-1), 'sample')  23.5 us
    all_to_all x1, blocking collectives, on_device(): lax.all_to_all(outgoing, 'expert', split_axis=0, concat_axis=0, tiled=True)  21.4 us
    convert_element_type x1, other arithmetic, on_device(): lax.psum(partial_sums.astype(jnp.bfloat16), 'sample').astype(jnp.float32)  12.4 us
    all_to_all x1, waiting for transfers between devices, on_device(): lax.all_to_all(finished, 'expert', split_axis=0, concat_axis=0, tiled=True)  11.9 us
  transfers between devices with their start and end apart: 4, of which 4 were waited for; matrix products, arithmetic and copies ran while one was open for 3% of the time, Pallas kernels for 0%

profile of v1, /device:TPU:97, one launch (start us, length us, event | category | flops | bytes accessed | tf_op | source)
XLA Modules:
  0.0 469.6 jit_solution(1622135046852311869)
XLA Ops:
  7.2 2.9 copy.81
  10.2 0.7 iota_compare_fusion.1
  10.9 1.1 slice_bitcast_fusion
  12.0 1.2 fusion.60
  13.2 94.0 %all-gather.2.cloned.1.call-done = bf16[8,1024,1024]{2,0,1:T(8,128)(2,1)} async-done(((bf16[8,64,1024]{2,0,1:T(8,128)(2,1)}), bf16[8,1024,1024]{2,0,1:T(8,128)(2,1)}) %all-gather.2.cloned.1.call-update) | async-done | bytes 16777232 | tf_op jit(solution)/shard_map/all_gather | solution.py:77
  107.3 11.3 %fusion.59 = (bf16[8,1024,512]{2,0,1:T(8,128)(2,1)}, bf16[8,1024,512]{2,0,1:T(8,128)(2,1)}) fusion(bf16[8,1024,1024]{2,0,1:T(8,128)(2,1)} %all-gather.2.cloned.1.call-done), kind=kLoop, calls=%fused_computation.80 | loop fusion | bytes 33554432 | tf_op jit(solution)/shard_map/slice | solution.py:35
  118.6 12.3 %copy.109 = bf16[8,1024,512]{1,2,0:T(8,128)(2,1)} copy(bf16[8,1024,512]{2,0,1:T(8,128)(2,1)} %get-tuple-element.8) | data formatting | bytes 16777216
  130.9 6.0 %bitcast_reduce_fusion = (f32[8,4,16]{2,1,0:T(4,128)S(1)}, f32[8,4,1024,16]{2,3,1,0:T(8,128)}) fusion(bf16[8,1024,4,128]{1,3,2,0:T(8,128)(2,1)} %bitcast.126, bf16[8,4,16,128]{3,0,2,1:T(8,128)(2,1)S(1)} %bitcast.132), kind=kOutput, calls=%fused_computation.15 | convolution fusion | flops 135265792 | bytes 10618880 | tf_op jit(solution)/shard_map/brhgd,bnhd->brhgn/dot_general | solution.py:41
  136.8 12.2 %copy.110 = bf16[8,1024,512]{1,2,0:T(8,128)(2,1)} copy(bf16[8,1024,512]{2,0,1:T(8,128)(2,1)} %get-tuple-element.9) | data formatting | bytes 16777216
  149.1 2.2 fusion.11
  151.4 9.0 %fusion.23 = f32[8,4,128,1,16]{2,4,1,0,3:T(8,128)S(1)} fusion(bf16[8,1024,4,128]{1,3,2,0:T(8,128)(2,1)} %bitcast.125, f32[8,4,1024,16]{2,3,1,0:T(8,128)S(1)} %copy-done.1, f32[8,4,16]{2,1,0:T(4,128)S(1)} %get-tuple-element.15), kind=kOutput, calls=%fused_computation.20 | convolution fusion | flops 806354944 | bytes 10749952 | tf_op jit(solution)/shard_map/brhgn,bnhd->brhgd/dot_general | solution.py:22
  161.2 1.5 stack.3
  162.7 5.2 %all-to-all-start = ((bf16[16,8,1,8192]{3,1,2,0:T(8,128)(2,1)}), bf16[16,8,1,8192]{3,1,2,0:T(8,128)(2,1)}, u32[]{:S(2)}, u32[]{:S(2)}) async-start(bf16[16,8,1,8192]{3,1,2,0:T(8,128)(2,1)} %stack.3), calls=%async_computation | async-start | bytes 4194304 | tf_op jit(solution)/shard_map/all_to_all | solution.py:87
  168.8 7.1 %gather_fusion.1 = s32[1024]{0:T(1024)S(1)} fusion(s32[128,48]{1,0:T(8,128)S(1)} %sub.53, s32[1024]{0:T(1024)S(1)} %reshape.316), kind=kCustom, calls=%fused_computation.1 | custom fusion | bytes 16384 | tf_op jit(solution)/shard_map/jit(take_along_axis)/gather | solution.py:110
  175.9 40.7 %all-to-all-done = bf16[16,8,1,8192]{3,1,2,0:T(8,128)(2,1)} async-done(((bf16[16,8,1,8192]{3,1,2,0:T(8,128)(2,1)}), bf16[16,8,1,8192]{3,1,2,0:T(8,128)(2,1)}, u32[]{:S(2)}, u32[]{:S(2)}) %all-to-all-start) | async-done | bytes 2097184 | tf_op jit(solution)/shard_map/all_to_all | solution.py:87
  216.7 3.6 multiply_reduce_fusion.1
  220.3 23.5 %psum.14 = f32[8,16]{0,1:T(8,128)S(1)} all-reduce(f32[8,16]{0,1:T(8,128)S(1)} %get-tuple-element.21), channel_id=1, replica_groups=mesh['sample'=16,'expert'=16] {'sample'}, use_global_device_ids=true, to_apply=%region_7.8 | all-reduce | flops 128 | bytes 1024 | tf_op jit(solution)/shard_map/psum | solution.py:94
  243.9 5.8 %scatter_custom_fusion = bf16[1248,256]{1,0:T(8,128)(2,1)} fusion(s32[1024]{0:T(1024)S(1)} %bitcast.134, bf16[]{:T(256)} %constant.35.clone.1, bf16[128,256]{1,0:T(8,128)(2,1)S(1)} %bitcast.129), kind=kCustom, calls=%fused_computation.37 | custom fusion | bytes 704514 | tf_op jit(solution)/shard_map/scatter | solution.py:115
  249.7 1.3 reshape.306
  251.0 21.4 %all_to_all.15 = bf16[16,3,26,256]{3,2,1,0:T(8,128)(2,1)S(1)} all-to-all(bf16[16,3,26,256]{3,2,1,0:T(8,128)(2,1)S(1)} %reshape.306), channel_id=1, replica_groups=mesh['sample'=16,'expert'=16] {'expert'}, dimensions={0} | all-to-all | bytes 1277952 | tf_op jit(solution)/shard_map/all_to_all | solution.py:120
  272.4 7.5 %convert_bitcast_fusion = bf16[16,3,26,3072]{3,2,0,1:T(8,128)(2,1)} fusion(bf16[3,256,3072]{2,1,0:T(8,128)(2,1)} %param.18, bf16[16,3,26,256]{3,2,1,0:T(8,128)(2,1)S(1)} %all_to_all.15), kind=kOutput, calls=%fused_computation.5 | convolution fusion | flops 1966768128 | bytes 13025280 | tf_op jit(solution)/shard_map/sjcd,jdf->sjcf/dot_general | solution.py:118
  279.9 134.1 %all-reduce.2.cloned.1.call-done = bf16[16,3,26,3072]{3,2,0,1:T(8,128)(2,1)} async-done(((bf16[16,3,26,3072]{3,2,0,1:T(8,128)(2,1)}), bf16[16,3,26,3072]{3,2,0,1:T(8,128)(2,1)}) %all-reduce.2.cloned.1.call-update) | async-done | bytes 7667728 | tf_op jit(solution)/shard_map/psum | solution.py:124
  414.0 12.4 %convert_element_type.49 = f32[16,3,26,3072]{3,2,0,1:T(8,128)} convert(bf16[16,3,26,3072]{3,2,0,1:T(8,128)(2,1)} %all-reduce.2.cloned.1.call-done) | non-fusion elementwise | flops 3833856 | bytes 23003136 | tf_op jit(solution)/shard_map/convert_element_type | solution.py:124
  426.4 8.0 %fusion.18 = bf16[16,3,26,256]{3,2,0,1:T(8,128)(2,1)S(1)} fusion(bf16[3,1536,256]{2,1,0:T(8,128)(2,1)S(1)} %copy-done, f32[16,3,26,3072]{3,2,0,1:T(8,128)} %convert_element_type.49), kind=kOutput, calls=%fused_computation.19 | convolution fusion | flops 993288192 | bytes 18333696 | tf_op jit(solution)/shard_map/sjcf,jfd->sjcd/dot_general | solution.py:126
  434.4 1.0 copy.99
  435.4 6.6 %all-to-all-start.2 = ((bf16[16,3,26,256]{3,2,1,0:T(8,128)(2,1)}), bf16[16,3,26,256]{3,2,1,0:T(8,128)(2,1)}, u32[]{:S(2)}, u32[]{:S(2)}) async-start(bf16[16,3,26,256]{3,2,1,0:T(8,128)(2,1)} %copy.99), calls=%async_computation.2 | async-start | bytes 1572864 | tf_op jit(solution)/shard_map/all_to_all | solution.py:129
  442.2 0.7 copy.107
  443.0 0.6 copy.102
  443.6 11.9 %all-to-all-done.2 = bf16[16,3,26,256]{3,2,1,0:T(8,128)(2,1)} async-done(((bf16[16,3,26,256]{3,2,1,0:T(8,128)(2,1)}), bf16[16,3,26,256]{3,2,1,0:T(8,128)(2,1)}, u32[]{:S(2)}, u32[]{:S(2)}) %all-to-all-start.2) | async-done | bytes 639008 | tf_op jit(solution)/shard_map/all_to_all | solution.py:129
  455.5 1.3 reshape.307
  456.8 3.9 gather_fusion
  460.8 1.9 multiply_reduce_fusion
  (44 shorter events, 2.2 us)
Async XLA Ops:
  7.2 419.2 %copy-start = (bf16[3,1536,256]{2,1,0:T(8,128)(2,1)S(1)}, bf16[3,1536,256]{2,1,0:T(8,128)(2,1)}, u32[]{:S(2)}) copy-start(bf16[3,1536,256]{2,1,0:T(8,128)(2,1)} %param.19) | copy-start | bytes 7077892
  7.2 100.1 %all-gather.2.cloned.1.call-start = ((), (), s32[]{:S(2)}) async-start(), calls=%async_computation.3 | async-start | bytes 17825792 | tf_op jit(solution)/shard_map/all_gather | solution.py:77
  118.6 12.3 %copy-start.3 = (bf16[8,1,8192]{2,0,1:T(8,128)(2,1)S(1)}, bf16[8,1,8192]{2,0,1:T(8,128)(2,1)}, u32[]{:S(2)}) copy-start(bf16[8,1,8192]{2,0,1:T(8,128)(2,1)} %param.11) | copy-start | bytes 393220
  149.1 2.3 copy-start.1
  160.4 7.5 %copy-start.4 = (s32[8,16,8]{1,2,0:T(8,128)S(1)}, s32[8,16,8]{1,2,0:T(8,128)}, u32[]{:S(2)}) copy-start(s32[8,16,8]{1,2,0:T(8,128)} %param.20) | copy-start | bytes 12292
  162.7 53.9 %all-to-all-start = ((bf16[16,8,1,8192]{3,1,2,0:T(8,128)(2,1)}), bf16[16,8,1,8192]{3,1,2,0:T(8,128)(2,1)}, u32[]{:S(2)}, u32[]{:S(2)}) async-start(bf16[16,8,1,8192]{3,1,2,0:T(8,128)(2,1)} %stack.3), calls=%async_computation | async-start | bytes 4194304 | tf_op jit(solution)/shard_map/all_to_all | solution.py:87
  167.9 246.1 %all-reduce.2.cloned.1.call-start = ((), (), s32[]{:S(2)}) async-start(), calls=%async_computation.4 | async-start | bytes 18874368 | tf_op jit(solution)/shard_map/psum | solution.py:124
  168.8 47.9 %copy-start.2 = (bf16[8,16,256]{2,1,0:T(8,128)(2,1)S(1)}, bf16[8,16,256]{2,1,0:T(8,128)(2,1)}, u32[]{:S(2)}) copy-start(bf16[8,16,256]{2,1,0:T(8,128)(2,1)} %param.16) | copy-start | bytes 196612
  175.9 67.9 %copy-start.6 = (f32[256]{0:T(256)S(1)}, f32[256]{0:T(256)}, u32[]{:S(2)}) copy-start(f32[256]{0:T(256)} %param.17) | copy-start | bytes 3076
  426.4 15.8 %copy-start.5 = (f32[8,16,8]{1,2,0:T(8,128)S(1)}, f32[8,16,8]{1,2,0:T(8,128)}, u32[]{:S(2)}) copy-start(f32[8,16,8]{1,2,0:T(8,128)} %param.21) | copy-start | bytes 12292
  435.4 20.2 %all-to-all-start.2 = ((bf16[16,3,26,256]{3,2,1,0:T(8,128)(2,1)}), bf16[16,3,26,256]{3,2,1,0:T(8,128)(2,1)}, u32[]{:S(2)}, u32[]{:S(2)}) async-start(bf16[16,3,26,256]{3,2,1,0:T(8,128)(2,1)} %copy.99), calls=%async_computation.2 | async-start | bytes 1572864 | tf_op jit(solution)/shard_map/all_to_all | solution.py:129
Sparse Core Ops, SparseCore 0:
  10.3 96.8 all-gather.1
  280.0 133.9 all-reduce.1
